TPU v7x, 32 devices: a whole 2x2x4 slice. The times are simulated.
32 devices in a mesh: grp: 4 (over y, x), body: 8 (over z, core).
Axes of the slice: x: 2, y: 2, z: 4, core: 2. Of those that a mesh axis runs over, the one named last changes fastest.
Arguments:
- incident: bfloat16 [32, 16, 512], P(('grp', 'body')), may hold values from -6 to 6
- exciting: float32 [32, 16, 512], P(('grp', 'body')), may hold values from -6 to 6
- t_matrices: bfloat16 [32, 2, 256, 256], P(('grp', 'body')), may hold values from -0.1875 to 0.1875
- hankel_rows: bfloat16 [225, 2, 512], replicated, may hold values from -0.09375 to 0.09375
- offsets: int32 [32, 8], P(('grp', 'body')), may hold values from 0 to 224
- lattice_slots: int32 [32], P('grp'), may hold values from 0 to 7, as said below
- up_maps: bfloat16 [32, 2, 256, 512], P(('grp', 'body')), may hold values from -0.125 to 0.125
- down_maps: bfloat16 [32, 2, 512, 256], P(('grp', 'body')), may hold values from -0.1875 to 0.1875
- group_maps: bfloat16 [4, 4, 2, 512, 512], P('grp', None, None, 'body'), may hold values from -0.09375 to 0.09375
Outputs:
- updated: float32 [32, 16, 512], P(('grp', 'body'))
Inputs may be any that keep to these rules, and one draw needn't show every extreme that they name: `lattice_slots`: within each group the 8 columns stand at the slots 0 to 7, one column a slot.
All inputs are finite; a program needn't handle non-finite values.
Results may differ from a plain program's by a relative error of at most 0.0034.
Values may be sent and summed in bfloat16 or wider, within the bound.
No kernel may reach another device: no remote copies, remote signals or barrier semaphores. Data moves between devices by JAX's collectives and lax.ppermute only.
A program may use at most 64 MiB of HBM per device.

v0:
```python
import math
import jax
import jax.numpy as jnp
from jax import lax
from jax.sharding import PartitionSpec as P


def complex_apply(form, values, real_mats, imag_mats):
    half_width = values.shape[-1] // 2
    real_values = values[..., :half_width]
    imag_values = values[..., half_width:]
    real_out = jnp.einsum(
        form, real_values, real_mats, preferred_element_type=jnp.float32
    ) - jnp.einsum(form, imag_values, imag_mats, preferred_element_type=jnp.float32)
    imag_out = jnp.einsum(
        form, real_values, imag_mats, preferred_element_type=jnp.float32
    ) + jnp.einsum(form, imag_values, real_mats, preferred_element_type=jnp.float32)
    return jnp.concatenate([real_out, imag_out], axis=-1)


def toeplitz_mats(sequences):
    length = sequences.shape[-1] // 2
    repeats = (1,) * (sequences.ndim - 1) + (length,)
    tiled = jnp.tile(sequences, repeats)
    window = tiled[..., length : length + length * (2 * length - 1)]
    return window.reshape(sequences.shape[:-1] + (length, 2 * length - 1))[..., :length]


def local(
    incident,
    exciting,
    t_matrices,
    hankel_rows,
    offsets,
    lattice_slots,
    up_maps,
    down_maps,
    group_maps,
):
    body_index = lax.axis_index("body")
    group_index = lax.axis_index("grp")
    local_count = incident.shape[0]
    scattered = complex_apply("iln,inm->ilm", incident, t_matrices[:, 0], t_matrices[:, 1]).astype(
        jnp.bfloat16
    )
    own_members = body_index * local_count + jnp.arange(local_count, dtype=jnp.int32)
    zero_seq = jnp.zeros((), jnp.bfloat16)
    empty = jnp.zeros(scattered.shape, jnp.float32)
    total = empty
    piece = lax.all_gather(scattered, "body", axis=0, tiled=True)
    width = piece.shape[0]
    block_rows = math.gcd(width, 4)
    table_rows = jnp.take(offsets, lattice_slots, axis=1)
    sequences = jnp.take(hankel_rows, table_rows, axis=0)
    sources = jnp.arange(width, dtype=jnp.int32)
    keep = own_members[:, None] != sources[None, :]
    sequences = jnp.where(keep[:, :, None, None], sequences, zero_seq)
    sequences = sequences.reshape(
        (local_count, width // block_rows, block_rows) + sequences.shape[2:]
    ).swapaxes(0, 1)
    pieces = piece.reshape((width // block_rows, block_rows) + piece.shape[1:])

    def one_block(accum, inputs):
        block_seqs, block_piece = inputs
        mats = toeplitz_mats(block_seqs)
        return (
            accum + complex_apply("jln,tjnm->tlm", block_piece, mats[:, :, 0], mats[:, :, 1]),
            None,
        )

    total, _ = lax.scan(one_block, total, (sequences, pieces))
    partial_value = complex_apply("iln,inq->lq", scattered, up_maps[:, 0], up_maps[:, 1])
    expansion = lax.psum(partial_value, "body").astype(jnp.bfloat16)
    block_width = group_maps.shape[3]
    full_width = group_maps.shape[4]
    real_block = lax.dynamic_slice_in_dim(expansion, body_index * block_width, block_width, 1)
    imag_block = lax.dynamic_slice_in_dim(
        expansion, full_width + body_index * block_width, block_width, 1
    )
    own_block = jnp.concatenate([real_block, imag_block], axis=-1)[None]
    piece = lax.all_gather(own_block, "grp", axis=0, tiled=True)
    width = piece.shape[0]
    sources = jnp.arange(width, dtype=jnp.int32)
    piece = jnp.where((sources != group_index)[:, None, None], piece, zero_seq)
    mats = group_maps[0]
    incoming_part = complex_apply("hln,hnq->lq", piece, mats[:, 0], mats[:, 1])
    incoming = lax.psum(incoming_part, "body").astype(jnp.bfloat16)
    far = complex_apply("lq,iqp->ilp", incoming, down_maps[:, 0], down_maps[:, 1])
    return exciting + total + far


def solution(mesh):
    return jax.shard_map(
        local,
        mesh=mesh,
        in_specs=(
            P(("grp", "body"), None, None),
            P(("grp", "body"), None, None),
            P(("grp", "body"), None, None, None),
            P(),
            P(("grp", "body"), None),
            P("grp"),
            P(("grp", "body"), None, None, None),
            P(("grp", "body"), None, None, None),
            P("grp", None, None, "body", None),
        ),
        out_specs=P(("grp", "body"), None, None),
        check_vma=False,
    )
```

profile of v0, /device:TPU:0, one launch (start us, length us, event | category | flops | bytes accessed | tf_op | source)
XLA Modules:
  0.0 120.4 jit_solution(14881951126355513148)
XLA Ops:
  0.0 0.0 copy-start
  0.0 0.0 copy-start.3
  0.0 1.1 fusion.38
  1.1 1.1 fusion.12
  2.2 1.1 fusion.20
  3.3 0.0 copy-start.2
  3.3 1.1 fusion.34
  4.5 1.1 fusion.13
  5.5 1.1 convolution_add_fusion
  6.6 1.1 fusion.24
  7.7 1.1 convolution_subtract_fusion
  8.8 0.0 copy-start.5
  8.9 0.0 copy-start.1
  8.9 30.7 %psum.14 = bf16[16,1024]{1,0:T(8,128)(2,1)S(1)} all-reduce(f32[16,1024]{1,0:T(8,128)S(1)} %pad_maximum_fusion), channel_id=1, replica_groups=mesh['grp'=4,'body'=8] {'body'}, use_global_device_ids=true, to_apply=%region_2.3 | all-reduce | flops 16384 | bytes 98304 | tf_op jit(solution)/shard_map/psum | solution.py:73
  39.6 0.1 constant_dynamic-slice_fusion.1
  39.7 0.1 pad_maximum_fusion.3
  39.8 8.2 %all-gather = bf16[64,128]{1,0:T(8,128)(2,1)S(1)} all-gather(bf16[16,128]{1,0:T(8,128)(2,1)S(1)} %pad_maximum_fusion.3), channel_id=2, replica_groups=mesh['grp'=4,'body'=8] {'grp'}, dimensions={0}, use_global_device_ids=true | all-gather | bytes 20480 | tf_op jit(solution)/shard_map/all_gather | solution.py:81
  48.0 0.1 broadcast_select_fusion.2
  48.0 0.0 copy-done.3
  48.1 0.2 convolution_bitcast_fusion.7
  48.3 0.3 fusion.9
  48.5 0.2 convolution_bitcast_fusion.5
  48.7 0.3 fusion.8
  49.0 26.3 %psum.15 = bf16[16,1024]{1,0:T(8,128)(2,1)S(1)} all-reduce(f32[16,1024]{1,0:T(8,128)S(1)} %pad_maximum_fusion.1), channel_id=1, replica_groups=mesh['grp'=4,'body'=8] {'body'}, use_global_device_ids=true, to_apply=%region_3.4 | all-reduce | flops 16384 | bytes 98304 | tf_op jit(solution)/shard_map/psum | solution.py:87
  75.3 0.0 copy-done.2
  75.3 0.1 fusion.18
  75.5 0.2 fusion.11
  75.6 0.2 fusion.14
  75.8 0.2 fusion.10
  75.9 14.0 %all_gather.6 = bf16[8,16,512]{2,1,0:T(8,128)(2,1)S(1)} all-gather(bf16[1,16,512]{2,1,0:T(8,128)(2,1)S(1)} %pad_maximum_fusion.2), channel_id=1, replica_groups=mesh['grp'=4,'body'=8] {'body'}, dimensions={0}, use_global_device_ids=true | all-gather | bytes 147456 | tf_op jit(solution)/shard_map/all_gather | solution.py:50
  89.9 0.0 copy-done.5
  89.9 0.0 copy-done.1
  89.9 0.6 gather_fusion
  90.6 0.0 copy-done
  90.6 0.6 gather_fusion.1
  91.2 0.1 broadcast_in_dim.54
  91.3 0.1 fusion.44
  91.4 0.0 copy-start.4
  91.4 28.3 %while.11 = (s32[]{:T(128)}, f32[1,16,512]{2,1,0:T(8,128)S(1)}, bf16[2,1,4,2,512]{4,3,2,1,0:T(2,128)(2,1)S(1)}, bf16[2,4,16,512]{3,2,1,0:T(8,128)(2,1)S(1)}, s32[]{:T(128)}, /*index=5*/s32[]{:T(128)}) while((s32[]{:T(128)}, f32[1,16,512]{2,1,0:T(8,128)S(1)}, bf16[2,1,4,2,512]{4,3,2,1,0:T(2,128)(2,1)S(1)}, ...), condition=%wide.region_1.2_spmd.clone, body=%wide.region_0.1_spmd.clone.sunk | while | flops 33587200 | bytes 17244244 | solution.py:71
  91.5 0.2 tile.16
  91.6 2.8 %tile.17 = bf16[1,4,2,131072]{3,2,1,0:T(2,128)(2,1)} reshape(bf16[4,2,256,512]{3,2,1,0:T(8,128)(2,1)S(1)} %tile.16) | data formatting | bytes 4194304 | tf_op jit(solution)/shard_map/while/body/eval_jaxpr/tile | solution.py:24
  94.4 4.3 %slice.213 = bf16[1,4,2,130816]{3,2,1,0:T(2,128)(2,1)} slice(bf16[1,4,2,131072]{3,2,1,0:T(2,128)(2,1)} %tile.17), slice={[0:1], [0:4], [0:2], [256:131072]} | slice | bytes 4186112 | tf_op jit(solution)/shard_map/while/body/eval_jaxpr/slice | solution.py:25
  98.7 6.1 %reshape.255 = bf16[1,4,2,256,511]{4,3,2,1,0:T(8,128)(2,1)S(1)} reshape(bf16[1,4,2,130816]{3,2,1,0:T(2,128)(2,1)} %slice.213) | data formatting | bytes 4186112 | tf_op jit(solution)/shard_map/while/body/eval_jaxpr/reshape | solution.py:26
  104.8 0.2 convolution_bitcast_fusion.11
  105.0 0.2 fusion.76
  105.2 0.2 convolution_bitcast_fusion.10
  105.4 0.2 fusion.75
  105.6 0.2 tile.16
  105.8 2.8 %tile.17 = bf16[1,4,2,131072]{3,2,1,0:T(2,128)(2,1)} reshape(bf16[4,2,256,512]{3,2,1,0:T(8,128)(2,1)S(1)} %tile.16) | data formatting | bytes 4194304 | tf_op jit(solution)/shard_map/while/body/eval_jaxpr/tile | solution.py:24
  108.5 4.3 %slice.213 = bf16[1,4,2,130816]{3,2,1,0:T(2,128)(2,1)} slice(bf16[1,4,2,131072]{3,2,1,0:T(2,128)(2,1)} %tile.17), slice={[0:1], [0:4], [0:2], [256:131072]} | slice | bytes 4186112 | tf_op jit(solution)/shard_map/while/body/eval_jaxpr/slice | solution.py:25
  112.9 6.1 %reshape.255 = bf16[1,4,2,256,511]{4,3,2,1,0:T(8,128)(2,1)S(1)} reshape(bf16[1,4,2,130816]{3,2,1,0:T(2,128)(2,1)} %slice.213) | data formatting | bytes 4186112 | tf_op jit(solution)/shard_map/while/body/eval_jaxpr/reshape | solution.py:26
  119.0 0.2 convolution_bitcast_fusion.11
  119.2 0.2 fusion.76
  119.4 0.2 convolution_bitcast_fusion.10
  119.6 0.2 fusion.75
  119.8 0.0 copy-done.4
  119.8 0.6 maximum_add_fusion.1
  (17 shorter events, 0.2 us)
Async XLA Ops:
  0.0 90.6 %copy-start = (bf16[225,2,512]{2,1,0:T(2,128)(2,1)S(1)}, bf16[225,2,512]{2,1,0:T(2,128)(2,1)}, u32[]{:S(2)}) copy-start(bf16[225,2,512]{2,1,0:T(2,128)(2,1)} %param.14) | copy-start | bytes 1382404
  0.0 48.0 %copy-start.3 = (bf16[1,4,2,64,512]{4,3,2,1,0:T(8,128)(2,1)S(1)}, bf16[1,4,2,64,512]{4,3,2,1,0:T(8,128)(2,1)}, u32[]{:S(2)}) copy-start(bf16[1,4,2,64,512]{4,3,2,1,0:T(8,128)(2,1)} %param.19) | copy-start | bytes 1572868
  3.3 72.0 %copy-start.2 = (bf16[1,2,512,256]{3,2,1,0:T(8,128)(2,1)S(1)}, bf16[1,2,512,256]{3,2,1,0:T(8,128)(2,1)}, u32[]{:S(2)}) copy-start(bf16[1,2,512,256]{3,2,1,0:T(8,128)(2,1)} %param.18) | copy-start | bytes 1572868
  8.8 81.1 %copy-start.5 = (s32[8]{0:T(128)S(1)}, s32[8]{0:T(128)}, u32[]{:S(2)}) copy-start(s32[8]{0:T(128)} %param.16) | copy-start | bytes 100
  8.9 81.1 %copy-start.1 = (s32[1,8]{1,0:T(1,128)S(1)}, s32[1,8]{1,0:T(1,128)}, u32[]{:S(2)}) copy-start(s32[1,8]{1,0:T(1,128)} %param.15) | copy-start | bytes 100
  91.4 28.4 %copy-start.4 = (f32[1,16,512]{2,1,0:T(8,128)S(1)}, f32[1,16,512]{2,1,0:T(8,128)}, u32[]{:S(2)}) copy-start(f32[1,16,512]{2,1,0:T(8,128)} %param.12) | copy-start | bytes 98308
where the time goes:
time: 121 us; the launch traced here: 120 us
  blocking collectives  79.2 us (65%)
  local copies, waits for them, and re-layouts  28.2 us (23%)
  matrix products  11.8 us (10%)
    psum x1, blocking collectives, local(): expansion = lax.psum(partial_value, 'body').astype(jnp.bfloat16)  30.7 us
    psum x1, blocking collectives, local(): incoming = lax.psum(incoming_part, 'body').astype(jnp.bfloat16)  26.3 us
    all_gather x1, blocking collectives, local(): piece = lax.all_gather(scattered, 'body', axis=0, tiled=True)  14 us
    reshape x2, local copies, waits for them, and re-layouts, toeplitz_mats(): window.reshape(sequences.shape[:-1] + (length, 2 * length - 1))  12.2 us
    slice x2, local copies, waits for them, and re-layouts, toeplitz_mats(): window = tiled[..., length:length + length * (2 * length - 1)]  8.67 us
    all_gather x1, blocking collectives, local(): piece = lax.all_gather(own_block, 'grp', axis=0, tiled=True)  8.18 us
    another operation x6, local copies, waits for them, and re-layouts, toeplitz_mats(): tiled = jnp.tile(sequences, repeats)  5.85 us
    dot_general x6, matrix products, complex_apply(): jnp.einsum(form, imag_values, real_mats, preferred_element_type=jnp.float32)  2.97 us

commit v1 on v0

--- a/solution.py
+++ b/solution.py
@@ -84,7 +84,7 @@
     piece = jnp.where((sources != group_index)[:, None, None], piece, zero_seq)
     mats = group_maps[0]
     incoming_part = complex_apply("hln,hnq->lq", piece, mats[:, 0], mats[:, 1])
-    incoming = lax.psum(incoming_part, "body").astype(jnp.bfloat16)
+    incoming = jnp.sum(lax.all_gather(incoming_part, "body"), axis=0).astype(jnp.bfloat16)
     far = complex_apply("lq,iqp->ilp", incoming, down_maps[:, 0], down_maps[:, 1])
     return exciting + total + far
 

time: 121 us -> 110 us (0.909)
  blocking collectives: 79.2 us -> 67.8 us
    psum x1 -> x0, blocking collectives: 26.3 us -> none  [local(): incoming = lax.psum(incoming_part, 'body').astype(jnp.bfloat16)]
    all_gather x0 -> x1, blocking collectives: none -> 14.9 us  [local(): lax.all_gather(incoming_part, 'body')]
where the time goes in v1:
time: 110 us; the launch traced here: 109 us
  blocking collectives  67.8 us (62%)
  local copies, waits for them, and re-layouts  28.2 us (26%)
  matrix products  11.8 us (11%)
    psum x1, blocking collectives, local(): expansion = lax.psum(partial_value, 'body').astype(jnp.bfloat16)  30.7 us
    all_gather x1, blocking collectives, local(): lax.all_gather(incoming_part, 'body')  14.9 us
    all_gather x1, blocking collectives, local(): piece = lax.all_gather(scattered, 'body', axis=0, tiled=True)  14 us
    reshape x2, local copies, waits for them, and re-layouts, toeplitz_mats(): window.reshape(sequences.shape[:-1] + (length, 2 * length - 1))  12.2 us
    slice x2, local copies, waits for them, and re-layouts, toeplitz_mats(): window = tiled[..., length:length + length * (2 * length - 1)]  8.67 us
    all_gather x1, blocking collectives, local(): piece = lax.all_gather(own_block, 'grp', axis=0, tiled=True)  8.18 us
    another operation x6, local copies, waits for them, and re-layouts, toeplitz_mats(): tiled = jnp.tile(sequences, repeats)  5.85 us
    dot_general x6, matrix products, complex_apply(): jnp.einsum(form, imag_values, imag_mats, preferred_element_type=jnp.float32)  3.02 us

profile of v1, /device:TPU:0, one launch (start us, length us, event | category | flops | bytes accessed | tf_op | source)
XLA Modules:
  0.0 109.0 jit_solution(8011051680875258858)
XLA Ops:
  0.0 0.0 copy-start
  0.0 0.0 copy-start.3
  0.0 1.1 %fusion.38 = f32[16,256]{1,0:T(8,128)S(1)} fusion(bf16[1,2,256,256]{3,2,1,0:T(8,128)(2,1)} %param.13, bf16[1,16,512]{2,1,0:T(8,128)(2,1)} %param.11), kind=kOutput, calls=%fused_computation.62 | convolution fusion | flops 2097152 | bytes 155648 | tf_op jit(solution)/shard_map/iln,inm->ilm/dot_general | solution.py:12
  1.1 1.1 fusion.12
  2.2 1.1 %fusion.20 = f32[16,512]{1,0:T(8,128)S(1)} fusion(bf16[16,256]{1,0:T(8,128)(2,1)S(1)} %fusion.12, bf16[1,2,256,512]{3,2,1,0:T(8,128)(2,1)} %param.17), kind=kOutput, calls=%fused_computation.44 | convolution fusion | flops 4194304 | bytes 303104 | tf_op jit(solution)/shard_map/iln,inq->lq/dot_general | solution.py:15
  3.3 1.1 fusion.34
  4.4 1.1 fusion.13
  5.5 1.1 %convolution_add_fusion = f32[16,512]{1,0:T(8,128)S(1)} fusion(f32[16,512]{1,0:T(8,128)S(1)} %fusion.20, bf16[16,256]{1,0:T(8,128)(2,1)S(1)} %fusion.13, bf16[1,2,256,512]{3,2,1,0:T(8,128)(2,1)} %param.17), kind=kOutput, calls=%fused_computation.25 | convolution fusion | flops 4202496 | bytes 335872 | tf_op jit(solution)/shard_map/iln,inq->lq/dot_general | solution.py:17
  6.6 1.1 %fusion.24 = f32[16,512]{1,0:T(8,128)S(1)} fusion(bf16[16,256]{1,0:T(8,128)(2,1)S(1)} %fusion.12, bf16[1,2,256,512]{3,2,1,0:T(8,128)(2,1)} %param.17), kind=kOutput, calls=%fused_computation.48 | convolution fusion | flops 4194304 | bytes 303104 | tf_op jit(solution)/shard_map/iln,inq->lq/dot_general | solution.py:12
  7.7 0.0 copy-start.2
  7.7 1.2 %convolution_subtract_fusion = f32[16,512]{1,0:T(8,128)S(1)} fusion(f32[16,512]{1,0:T(8,128)S(1)} %fusion.24, bf16[16,256]{1,0:T(8,128)(2,1)S(1)} %fusion.13, bf16[1,2,256,512]{3,2,1,0:T(8,128)(2,1)} %param.17), kind=kOutput, calls=%fused_computation.26 | convolution fusion | flops 4202496 | bytes 335872 | tf_op jit(solution)/shard_map/iln,inq->lq/dot_general | solution.py:14
  8.8 30.7 %psum.7 = bf16[16,1024]{1,0:T(8,128)(2,1)S(1)} all-reduce(f32[16,1024]{1,0:T(8,128)S(1)} %pad_maximum_fusion), channel_id=1, replica_groups=mesh['grp'=4,'body'=8] {'body'}, use_global_device_ids=true, to_apply=%region_2.3 | all-reduce | flops 16384 | bytes 98304 | tf_op jit(solution)/shard_map/psum | solution.py:73
  39.6 0.1 constant_dynamic-slice_fusion.1
  39.7 0.1 pad_maximum_fusion.3
  39.8 8.2 %all-gather = bf16[64,128]{1,0:T(8,128)(2,1)S(1)} all-gather(bf16[16,128]{1,0:T(8,128)(2,1)S(1)} %pad_maximum_fusion.3), channel_id=2, replica_groups=mesh['grp'=4,'body'=8] {'grp'}, dimensions={0}, use_global_device_ids=true | all-gather | bytes 20480 | tf_op jit(solution)/shard_map/all_gather | solution.py:81
  47.9 0.1 broadcast_select_fusion.2
  48.0 0.0 copy-done.3
  48.1 0.0 copy-start.5
  48.1 0.0 copy-start.1
  48.1 0.2 convolution_bitcast_fusion.7
  48.3 0.3 fusion.9
  48.5 0.2 convolution_bitcast_fusion.5
  48.7 0.3 fusion.8
  49.0 14.9 %all-gather.1 = f32[128,1024]{1,0:T(8,128)S(1)} all-gather(f32[16,1024]{1,0:T(8,128)S(1)} %pad_maximum_fusion.1), channel_id=3, replica_groups=mesh['grp'=4,'body'=8] {'body'}, dimensions={0}, use_global_device_ids=true | all-gather | bytes 589824 | tf_op jit(solution)/shard_map/all_gather | solution.py:87
  64.0 0.0 copy-done.2
  64.0 0.1 fusion.18
  64.1 0.2 fusion.11
  64.3 0.2 fusion.14
  64.4 0.2 fusion.10
  64.6 14.0 %all_gather.12 = bf16[8,16,512]{2,1,0:T(8,128)(2,1)S(1)} all-gather(bf16[1,16,512]{2,1,0:T(8,128)(2,1)S(1)} %pad_maximum_fusion.2), channel_id=1, replica_groups=mesh['grp'=4,'body'=8] {'body'}, dimensions={0}, use_global_device_ids=true | all-gather | bytes 147456 | tf_op jit(solution)/shard_map/all_gather | solution.py:50
  78.5 0.0 copy-done.5
  78.6 0.0 copy-done.1
  78.6 0.6 gather_fusion
  79.3 0.0 copy-done
  79.3 0.6 gather_fusion.1
  79.9 0.1 broadcast_in_dim.54
  80.0 0.1 fusion.44
  80.1 0.0 copy-start.4
  80.1 28.3 %while.11 = (s32[]{:T(128)}, f32[1,16,512]{2,1,0:T(8,128)S(1)}, bf16[2,1,4,2,512]{4,3,2,1,0:T(2,128)(2,1)S(1)}, bf16[2,4,16,512]{3,2,1,0:T(8,128)(2,1)S(1)}, s32[]{:T(128)}, /*index=5*/s32[]{:T(128)}) while((s32[]{:T(128)}, f32[1,16,512]{2,1,0:T(8,128)S(1)}, bf16[2,1,4,2,512]{4,3,2,1,0:T(2,128)(2,1)S(1)}, ...), condition=%wide.region_1.2_spmd.clone, body=%wide.region_0.1_spmd.clone.sunk | while | flops 33587200 | bytes 17244244 | solution.py:71
  80.1 0.2 tile.16
  80.3 2.8 %tile.17 = bf16[1,4,2,131072]{3,2,1,0:T(2,128)(2,1)} reshape(bf16[4,2,256,512]{3,2,1,0:T(8,128)(2,1)S(1)} %tile.16) | data formatting | bytes 4194304 | tf_op jit(solution)/shard_map/while/body/eval_jaxpr/tile | solution.py:24
  83.0 4.3 %slice.213 = bf16[1,4,2,130816]{3,2,1,0:T(2,128)(2,1)} slice(bf16[1,4,2,131072]{3,2,1,0:T(2,128)(2,1)} %tile.17), slice={[0:1], [0:4], [0:2], [256:131072]} | slice | bytes 4186112 | tf_op jit(solution)/shard_map/while/body/eval_jaxpr/slice | solution.py:25
  87.4 6.1 %reshape.256 = bf16[1,4,2,256,511]{4,3,2,1,0:T(8,128)(2,1)S(1)} reshape(bf16[1,4,2,130816]{3,2,1,0:T(2,128)(2,1)} %slice.213) | data formatting | bytes 4186112 | tf_op jit(solution)/shard_map/while/body/eval_jaxpr/reshape | solution.py:26
  93.5 0.2 convolution_bitcast_fusion.11
  93.7 0.2 fusion.76
  93.8 0.2 convolution_bitcast_fusion.10
  94.0 0.2 fusion.75
  94.3 0.2 tile.16
  94.4 2.8 %tile.17 = bf16[1,4,2,131072]{3,2,1,0:T(2,128)(2,1)} reshape(bf16[4,2,256,512]{3,2,1,0:T(8,128)(2,1)S(1)} %tile.16) | data formatting | bytes 4194304 | tf_op jit(solution)/shard_map/while/body/eval_jaxpr/tile | solution.py:24
  97.2 4.3 %slice.213 = bf16[1,4,2,130816]{3,2,1,0:T(2,128)(2,1)} slice(bf16[1,4,2,131072]{3,2,1,0:T(2,128)(2,1)} %tile.17), slice={[0:1], [0:4], [0:2], [256:131072]} | slice | bytes 4186112 | tf_op jit(solution)/shard_map/while/body/eval_jaxpr/slice | solution.py:25
  101.5 6.1 %reshape.256 = bf16[1,4,2,256,511]{4,3,2,1,0:T(8,128)(2,1)S(1)} reshape(bf16[1,4,2,130816]{3,2,1,0:T(2,128)(2,1)} %slice.213) | data formatting | bytes 4186112 | tf_op jit(solution)/shard_map/while/body/eval_jaxpr/reshape | solution.py:26
  107.6 0.2 convolution_bitcast_fusion.11
  107.8 0.2 fusion.76
  108.0 0.2 convolution_bitcast_fusion.10
  108.2 0.2 fusion.75
  108.4 0.0 copy-done.4
  108.4 0.6 maximum_add_fusion.1
  (18 shorter events, 0.2 us)
Async XLA Ops:
  0.0 79.3 %copy-start = (bf16[225,2,512]{2,1,0:T(2,128)(2,1)S(1)}, bf16[225,2,512]{2,1,0:T(2,128)(2,1)}, u32[]{:S(2)}) copy-start(bf16[225,2,512]{2,1,0:T(2,128)(2,1)} %param.14) | copy-start | bytes 1382404
  0.0 48.0 %copy-start.3 = (bf16[1,4,2,64,512]{4,3,2,1,0:T(8,128)(2,1)S(1)}, bf16[1,4,2,64,512]{4,3,2,1,0:T(8,128)(2,1)}, u32[]{:S(2)}) copy-start(bf16[1,4,2,64,512]{4,3,2,1,0:T(8,128)(2,1)} %param.19) | copy-start | bytes 1572868
  7.7 56.3 %copy-start.2 = (bf16[1,2,512,256]{3,2,1,0:T(8,128)(2,1)S(1)}, bf16[1,2,512,256]{3,2,1,0:T(8,128)(2,1)}, u32[]{:S(2)}) copy-start(bf16[1,2,512,256]{3,2,1,0:T(8,128)(2,1)} %param.18) | copy-start | bytes 1572868
  48.1 30.5 %copy-start.5 = (s32[8]{0:T(128)S(1)}, s32[8]{0:T(128)}, u32[]{:S(2)}) copy-start(s32[8]{0:T(128)} %param.16) | copy-start | bytes 100
  48.1 30.5 %copy-start.1 = (s32[1,8]{1,0:T(1,128)S(1)}, s32[1,8]{1,0:T(1,128)}, u32[]{:S(2)}) copy-start(s32[1,8]{1,0:T(1,128)} %param.15) | copy-start | bytes 100
  80.1 28.4 %copy-start.4 = (f32[1,16,512]{2,1,0:T(8,128)S(1)}, f32[1,16,512]{2,1,0:T(8,128)}, u32[]{:S(2)}) copy-start(f32[1,16,512]{2,1,0:T(8,128)} %param.12) | copy-start | bytes 98308
